TPU v7x, 256 devices: a whole 4x4x8 slice. The times are simulated.
256 devices in a mesh: row: 8 (over y, core), col: 32 (over z, x).
Axes of the slice: x: 4, y: 4, z: 8, core: 2. Of those that a mesh axis runs over, the one named last changes fastest.
Arguments:
- amps: bfloat16 [1024, 256, 256], P('row', 'col'), may hold values from -6 to 6
- ints: bfloat16 [16384, 256, 256], P(('row', 'col')), may hold values from -0.0234375 to 0.0234375
- task_cd: int32 [16384], P(('row', 'col')), may hold values from 0 to 7, as said below
- task_ab: int32 [16384], P(('row', 'col')), may hold values from 0 to 7
- task_count: int32 [256], P(('row', 'col')), may hold values from 8 to 64, as said below
Outputs:
- residual: bfloat16 [1024, 64, 256], P('col', 'row')
Inputs may be any that keep to these rules, and one draw needn't show every extreme that they name: On each device the slots name distinct (task_cd, task_ab) pairs. The live slots of a device are its first task_count ones; some device has all 64 slots live in every draw.
All inputs are finite; a program needn't handle non-finite values.
Results may differ from a plain program's by a relative error of at most 0.001.
Values may be sent and summed in bfloat16 or wider, within the bound.
A program may use at most 128 MiB of HBM per device.

v0:
```python
import jax
import jax.numpy as jnp
from jax import lax
from jax.sharding import Mesh
from jax.sharding import PartitionSpec as P

CD_COL = 8
PAIR_TILES_ROW = 8
COL = ("col_0", "col_1")
ROW_COL = ("row", "col_0", "col_1")


def sum_by_axis(value, axes, dim):
    for axis in axes:
        value = lax.psum_scatter(value, axis, scatter_dimension=dim, tiled=True)
    return value


def dense_tiles(ints, task_cd, task_ab, count):
    slots = ints.shape[0]
    order = jnp.arange(slots, dtype=jnp.int32)
    live = order < count
    wanted = jnp.arange(PAIR_TILES_ROW * CD_COL, dtype=jnp.int32)[:, None]
    slot_key = task_ab * CD_COL + task_cd
    match = (slot_key[None, :] == wanted) & live[None, :]
    found = jnp.sum(jnp.where(match, order[None, :], 0), axis=1)
    present_mask = jnp.any(match, axis=1)
    table = jnp.take(ints, found, axis=0) * present_mask.astype(ints.dtype)[:, None, None]
    return table.reshape(PAIR_TILES_ROW, CD_COL, ints.shape[1], ints.shape[2])


def ladder_term(rows_amps, table):
    return jnp.einsum("nkt,aktu->nau", rows_amps, table, preferred_element_type=jnp.float32)


def shards(amps, ints, task_cd, task_ab, task_count):
    whole = lax.all_gather(amps, "row", axis=0, tiled=True)
    table = dense_tiles(ints, task_cd, task_ab, task_count[0])
    partial_sum = ladder_term(whole, table)
    summed = sum_by_axis(partial_sum, COL, 0)
    return summed.astype(jnp.bfloat16)


def solution(mesh):
    finer = Mesh(mesh.devices.reshape(mesh.shape["row"], 8, 4), ("row", "col_0", "col_1"))
    in_specs = (P("row", COL, None), P(ROW_COL, None, None), P(ROW_COL), P(ROW_COL), P(ROW_COL))
    out_specs = P(COL, "row", None)
    return jax.shard_map(
        shards, mesh=finer, in_specs=in_specs, out_specs=out_specs, check_vma=False
    )
```

profile of v0, /device:TPU:8, one launch (start us, length us, event | category | flops | bytes accessed | tf_op | source)
XLA Modules:
  0.0 192.2 jit_solution(13895775385929147668)
XLA Ops:
  6.5 0.0 all-gather.2.cloned.1.call-start
  6.5 1.9 %copy.13 = bf16[128,8,256]{2,0,1:T(8,128)(2,1)} copy(bf16[128,8,256]{2,1,0:T(8,128)(2,1)} %param.5) | data formatting | bytes 1048576 | tf_op args[0]
  8.5 0.0 all-gather.2.cloned.1.call-update
  8.5 0.0 reduce-scatter.3.cloned.1.call-start
  9.2 0.7 multiply_add_fusion
  9.9 0.1 fusion.13
  10.0 0.1 reshape.35
  10.1 0.1 select_reduce_fusion
  10.2 0.1 reduce_sum.14
  10.3 8.6 %gather_fusion = bf16[64,256,256]{2,1,0:T(8,128)(2,1)} fusion(bf16[64,256,256]{2,1,0:T(8,128)(2,1)} %param.6, s32[1024]{0:T(1024)S(1)} %pad_clamp_fusion), kind=kCustom, calls=%fused_computation | custom fusion | bytes 16777472 | tf_op jit(solution)/shard_map/jit(_take)/gather | solution.py:28
  19.0 11.6 %copy.12 = bf16[8,8,256,256]{2,3,1,0:T(8,128)(2,1)} copy(bf16[8,8,256,256]{3,2,1,0:T(8,128)(2,1)} %bitcast.17) | data formatting | bytes 16777216 | tf_op jit(solution)/shard_map/jit(_take)/gather | solution.py:28
  30.6 15.1 %all-gather.2.cloned.1.call-done = bf16[1024,8,256]{2,0,1:T(8,128)(2,1)} async-done(((bf16[128,8,256]{2,0,1:T(8,128)(2,1)}), bf16[1024,8,256]{2,0,1:T(8,128)(2,1)}) %all-gather.2.cloned.1.call-update) | async-done | bytes 4194320 | tf_op jit(solution)/shard_map/all_gather | solution.py:37
  45.7 14.5 %fusion.7 = f32[1024,8,256]{0,2,1:T(8,128)} fusion(bf16[1024,8,256]{2,0,1:T(8,128)(2,1)} %all-gather.2.cloned.1.call-done, bf16[8,8,256,256]{2,3,1,0:T(8,128)(2,1)} %copy.12, pred[8,8]{1,0:T(8,128)(4,1)S(1)} %compare_and_fusion, bf16[8,8]{1,0:T(8,128)(2,1)S(1)} %reshape.35), kind=kOutput, calls=%fused_computation.8 | convolution fusion | flops 8598323200 | bytes 20971712 | tf_op jit(solution)/shard_map/nkt,aktu->nau/dot_general | solution.py:33
  60.2 0.0 reduce-scatter.3.cloned.1.call-update
  60.2 0.0 reduce-scatter.5.cloned.1.call-start
  60.2 96.0 %reduce-scatter.3.cloned.1.call-done = f32[128,8,256]{0,2,1:T(8,128)} async-done(((f32[1024,8,256]{0,2,1:T(8,128)}), f32[128,8,256]{0,2,1:T(8,128)}) %reduce-scatter.3.cloned.1.call-update) | async-done | bytes 1048592 | tf_op jit(solution)/shard_map/reduce_scatter | solution.py:15
  156.3 2.7 %copy.14 = f32[128,8,256]{2,1,0:T(8,128)} copy(f32[128,8,256]{0,2,1:T(8,128)} %reduce-scatter.3.cloned.1.call-done) | data formatting | bytes 2097152 | tf_op jit(solution)/shard_map/reduce_scatter | solution.py:15
  158.9 0.0 reduce-scatter.5.cloned.1.call-update
  159.0 25.1 %reduce-scatter.5.cloned.1.call-done = f32[32,8,256]{2,1,0:T(8,128)} async-done(((f32[128,8,256]{2,1,0:T(8,128)}), f32[32,8,256]{2,1,0:T(8,128)}) %reduce-scatter.5.cloned.1.call-update) | async-done | bytes 262160 | tf_op jit(solution)/shard_map/reduce_scatter | solution.py:15
  184.0 1.6 convert_element_type.15
  (5 shorter events, 0.0 us)
Async XLA Ops:
  6.5 39.1 %all-gather.2.cloned.1.call-start = ((), (), s32[]{:S(2)}) async-start(), calls=%async_computation.2 | async-start | bytes 4718592 | tf_op jit(solution)/shard_map/all_gather | solution.py:37
  8.5 147.8 %reduce-scatter.3.cloned.1.call-start = ((), (), s32[]{:S(2)}) async-start(), calls=%async_computation.3 | async-start | bytes 9437184 | tf_op jit(solution)/shard_map/reduce_scatter | solution.py:15
  60.2 123.8 %reduce-scatter.5.cloned.1.call-start = ((), (), s32[]{:S(2)}) async-start(), calls=%async_computation.4 | async-start | bytes 1310720 | tf_op jit(solution)/shard_map/reduce_scatter | solution.py:15
Sparse Core Ops, SparseCore 0:
  9.2 36.4 all-gather.1
  60.3 95.9 reduce-scatter.2
  159.1 24.8 reduce-scatter.4
where the time goes:
time: 193 us; the launch traced here: 192 us
  waiting for transfers between devices  136 us (70%)
  local copies, waits for them, and re-layouts  25 us (13%)
  matrix products  14.5 us (8%)
  between operations  13.8 us (7%)
  other arithmetic  2.57 us (1%)
    reduce_scatter x2, waiting for transfers between devices, sum_by_axis(): value = lax.psum_scatter(value, axis, scatter_dimension=dim, tiled=True)  121 us
    gather x2, local copies, waits for them, and re-layouts, dense_tiles(): jnp.take(ints, found, axis=0)  20.3 us
    all_gather x1, waiting for transfers between devices, shards(): whole = lax.all_gather(amps, 'row', axis=0, tiled=True)  15.1 us
    dot_general x1, matrix products, ladder_term(): jnp.einsum('nkt,aktu->nau', rows_amps, table, preferred_element_type=jnp....  14.5 us
  transfers between devices with their start and end apart: 3, of which 3 were waited for; matrix products, arithmetic and copies ran while one was open for 11% of the time, Pallas kernels for 0%

commit v1 on v0

--- a/solution.py
+++ b/solution.py
@@ -34,7 +34,9 @@
 
 
 def shards(amps, ints, task_cd, task_ab, task_count):
-    whole = lax.all_gather(amps, "row", axis=0, tiled=True)
+    whole = jnp.concatenate(
+        lax.all_to_all(jnp.stack([amps] * lax.axis_size("row")), "row", 0, 0), axis=0
+    )
     table = dense_tiles(ints, task_cd, task_ab, task_count[0])
     partial_sum = ladder_term(whole, table)
     summed = sum_by_axis(partial_sum, COL, 0)

time: 193 us -> 213 us (1.10)
  waiting for transfers between devices: 136 us -> 151 us
  other arithmetic: 2.57 us -> 9.36 us
  starting transfers between devices: 0.09 us -> 6.68 us
  local copies, waits for them, and re-layouts: 25 us -> 19.6 us
  matrix products: 14.5 us -> 11.2 us
    all_to_all x0 -> x1, waiting for transfers between devices: none -> 31.2 us  [shards(): lax.all_to_all(jnp.stack([amps] * lax.axis_size('row')), 'row', 0, 0)]
    all_gather x1 -> x0, waiting for transfers between devices: 15.1 us -> none  [shards(): whole = lax.all_gather(amps, 'row', axis=0, tiled=True)]
    gather x2 -> x1, local copies, waits for them, and re-layouts: 20.3 us -> 8.66 us  [dense_tiles(): jnp.take(ints, found, axis=0)]
    mul x0 -> x1, other arithmetic: none -> 7.49 us  [dense_tiles(): jnp.take(ints, found, axis=0)]
    all_to_all x0 -> x1, starting transfers between devices: none -> 6.64 us  [shards(): lax.all_to_all(jnp.stack([amps] * lax.axis_size('row')), 'row', 0, 0)]
    dot_general x1, matrix products: 14.5 us -> 11.2 us  [ladder_term(): jnp.einsum('nkt,aktu->nau', rows_amps, table, preferred_element_type=jnp....]
    all_to_all x0 -> x1, local copies, waits for them, and re-layouts: none -> 2.61 us  [shards(): lax.all_to_all(jnp.stack([amps] * lax.axis_size('row')), 'row', 0, 0)]
    another operation x0 -> x1, local copies, waits for them, and re-layouts: none -> 2.49 us  [shards(): jnp.stack([amps] * lax.axis_size('row'))]
  transfers between devices with their start and end apart: 3 -> 3, of which waited for: 3 -> 3; matrix products, arithmetic and copies ran while one was open for 11% -> 8% of each run, Pallas kernels for 0% -> 0%
where the time goes in v1:
time: 213 us; the launch traced here: 212 us
  waiting for transfers between devices  151 us (71%)
  local copies, waits for them, and re-layouts  19.6 us (9%)
  between operations  14.1 us (7%)
  matrix products  11.2 us (5%)
  other arithmetic  9.36 us (4%)
  starting transfers between devices  6.68 us (3%)
    reduce_scatter x2, waiting for transfers between devices, sum_by_axis(): value = lax.psum_scatter(value, axis, scatter_dimension=dim, tiled=True)  120 us
    all_to_all x1, waiting for transfers between devices, shards(): lax.all_to_all(jnp.stack([amps] * lax.axis_size('row')), 'row', 0, 0)  31.2 us
    dot_general x1, matrix products, ladder_term(): jnp.einsum('nkt,aktu->nau', rows_amps, table, preferred_element_type=jnp....  11.2 us
    gather x1, local copies, waits for them, and re-layouts, dense_tiles(): jnp.take(ints, found, axis=0)  8.66 us
    mul x1, other arithmetic, dense_tiles(): jnp.take(ints, found, axis=0)  7.49 us
    all_to_all x1, starting transfers between devices, shards(): lax.all_to_all(jnp.stack([amps] * lax.axis_size('row')), 'row', 0, 0)  6.64 us
  transfers between devices with their start and end apart: 3, of which 3 were waited for; matrix products, arithmetic and copies ran while one was open for 8% of the time, Pallas kernels for 0%

profile of v1, /device:TPU:8, one launch (start us, length us, event | category | flops | bytes accessed | tf_op | source)
XLA Modules:
  0.0 212.4 jit_solution(1730093701405811569)
XLA Ops:
  6.5 0.0 copy-start.2
  6.5 0.0 copy-start.1
  6.5 1.2 copy.13
  7.7 2.5 %stack.2 = bf16[8,128,8,256]{3,1,2,0:T(8,128)(2,1)} broadcast(bf16[128,8,256]{2,0,1:T(8,128)(2,1)S(1)} %copy.13), dimensions={1,2,3} | broadcast | bytes 4718592 | tf_op jit(solution)/shard_map/stack | solution.py:38
  10.2 6.6 %all-to-all-start = ((bf16[8,128,8,256]{3,1,2,0:T(8,128)(2,1)}), bf16[8,128,8,256]{3,1,2,0:T(8,128)(2,1)}, u32[]{:S(2)}, u32[]{:S(2)}) async-start(bf16[8,128,8,256]{3,1,2,0:T(8,128)(2,1)} %stack.2), calls=%async_computation | async-start | bytes 8388608 | tf_op jit(solution)/shard_map/all_to_all | solution.py:38
  16.8 0.0 reduce-scatter.3.cloned.1.call-start
  17.5 0.0 copy-done.2
  17.5 0.0 copy-done.1
  17.5 0.1 fusion.1
  17.7 0.1 select_reduce_fusion
  17.8 8.7 %gather_fusion = bf16[64,256,256]{2,1,0:T(8,128)(2,1)} fusion(bf16[64,256,256]{2,1,0:T(8,128)(2,1)} %param.6, s32[1024]{0:T(1024)S(1)} %pad_clamp_fusion), kind=kCustom, calls=%fused_computation | custom fusion | bytes 16777472 | tf_op jit(solution)/shard_map/jit(_take)/gather | solution.py:28
  26.5 7.5 %select_multiply_fusion = bf16[64,256,256]{2,1,0:T(8,128)(2,1)} fusion(bf16[64,256,256]{2,1,0:T(8,128)(2,1)} %gather_fusion, pred[64]{0:T(512)(128)(4,1)S(1)} %compare_and_fusion, bf16[64]{0:T(256)(128)(2,1)S(1)} %convert_element_type.10), kind=kLoop, calls=%fused_computation.1 | loop fusion | flops 8388608 | bytes 16777408 | tf_op jit(solution)/shard_map/mul | solution.py:28
  34.0 31.2 %all-to-all-done = bf16[8,128,8,256]{3,1,2,0:T(8,128)(2,1)} async-done(((bf16[8,128,8,256]{3,1,2,0:T(8,128)(2,1)}), bf16[8,128,8,256]{3,1,2,0:T(8,128)(2,1)}, u32[]{:S(2)}, u32[]{:S(2)}) %all-to-all-start) | async-done | bytes 4194336 | tf_op jit(solution)/shard_map/all_to_all | solution.py:38
  65.2 0.0 copy-start
  65.2 2.6 %copy.14 = bf16[8,128,8,256]{3,1,0,2:T(8,128)(2,1)S(1)} copy(bf16[8,128,8,256]{3,1,2,0:T(8,128)(2,1)} %all-to-all-done) | data formatting | bytes 8388608 | tf_op jit(solution)/shard_map/all_to_all | solution.py:38
  67.8 2.0 copy-done
  69.8 11.2 %convolution_bitcast_fusion = f32[1024,8,256]{0,2,1:T(8,128)} fusion(bf16[8,8,256,256]{3,2,1,0:T(8,128)(2,1)S(1)} %bitcast.17, bf16[1024,8,256,1]{2,0,1,3:T(8,128)(2,1)S(1)} %bitcast.18), kind=kOutput, calls=%fused_computation.2 | convolution fusion | flops 8589934592 | bytes 20971520 | tf_op jit(solution)/shard_map/nkt,aktu->nau/dot_general | solution.py:33
  81.0 0.0 reduce-scatter.3.cloned.1.call-update
  81.0 0.0 reduce-scatter.5.cloned.1.call-start
  81.1 95.2 %reduce-scatter.3.cloned.1.call-done = f32[128,8,256]{0,2,1:T(8,128)} async-done(((f32[1024,8,256]{0,2,1:T(8,128)}), f32[128,8,256]{0,2,1:T(8,128)}) %reduce-scatter.3.cloned.1.call-update) | async-done | bytes 1048592 | tf_op jit(solution)/shard_map/reduce_scatter | solution.py:15
  176.3 2.6 %copy.16 = f32[128,8,256]{2,1,0:T(8,128)} copy(f32[128,8,256]{0,2,1:T(8,128)} %reduce-scatter.3.cloned.1.call-done) | data formatting | bytes 2097152 | tf_op jit(solution)/shard_map/reduce_scatter | solution.py:15
  178.9 0.0 reduce-scatter.5.cloned.1.call-update
  178.9 25.1 %reduce-scatter.5.cloned.1.call-done = f32[32,8,256]{2,1,0:T(8,128)} async-done(((f32[128,8,256]{2,1,0:T(8,128)}), f32[32,8,256]{2,1,0:T(8,128)}) %reduce-scatter.5.cloned.1.call-update) | async-done | bytes 262160 | tf_op jit(solution)/shard_map/reduce_scatter | solution.py:15
  204.0 1.6 convert_element_type.11
  (6 shorter events, 0.0 us)
Async XLA Ops:
  6.5 11.0 %copy-start.2 = (s32[64]{0:T(128)S(1)}, s32[64]{0:T(128)}, u32[]{:S(2)}) copy-start(s32[64]{0:T(128)} %param.8) | copy-start | bytes 772
  6.5 11.0 %copy-start.1 = (s32[64]{0:T(128)S(1)}, s32[64]{0:T(128)}, u32[]{:S(2)}) copy-start(s32[64]{0:T(128)} %param.7) | copy-start | bytes 772
  10.2 55.0 %all-to-all-start = ((bf16[8,128,8,256]{3,1,2,0:T(8,128)(2,1)}), bf16[8,128,8,256]{3,1,2,0:T(8,128)(2,1)}, u32[]{:S(2)}, u32[]{:S(2)}) async-start(bf16[8,128,8,256]{3,1,2,0:T(8,128)(2,1)} %stack.2), calls=%async_computation | async-start | bytes 8388608 | tf_op jit(solution)/shard_map/all_to_all | solution.py:38
  16.8 159.4 %reduce-scatter.3.cloned.1.call-start = ((), (), s32[]{:S(2)}) async-start(), calls=%async_computation.3 | async-start | bytes 9437184 | tf_op jit(solution)/shard_map/reduce_scatter | solution.py:15
  65.2 4.6 %copy-start = (bf16[64,256,256]{2,1,0:T(8,128)(2,1)S(1)}, bf16[64,256,256]{2,1,0:T(8,128)(2,1)}, u32[]{:S(2)}) copy-start(bf16[64,256,256]{2,1,0:T(8,128)(2,1)} %select_multiply_fusion) | copy-start | bytes 25165828
  81.0 122.9 %reduce-scatter.5.cloned.1.call-start = ((), (), s32[]{:S(2)}) async-start(), calls=%async_computation.4 | async-start | bytes 1310720 | tf_op jit(solution)/shard_map/reduce_scatter | solution.py:15
Sparse Core Ops, SparseCore 0:
  81.2 95.0 reduce-scatter.2
  179.0 24.8 reduce-scatter.4
